TPU v7x, 32 devices: a whole 2x2x4 slice. The times are simulated.
32 devices in a mesh: parts: 2 (over y), dp: 4 (over z), tensor: 2 (over x), group: 2 (over core).
Axes of the slice: x: 2, y: 2, z: 4, core: 2. Of those that a mesh axis runs over, the one named last changes fastest.
Arguments:
- activations: bfloat16 [1, 32, 256, 4096], P(None, ('parts', 'dp'), None, ('tensor', 'group')), parts along dimension 1, may hold values from -6 to 6
- out_grads: bfloat16 [1, 32, 256, 14336], P(None, ('parts', 'dp'), None, ('tensor', 'group')), parts along dimension 1, may hold values from -6 to 6
- proj_in: bfloat16 [1, 4096, 64], P(None, ('tensor', 'group')), may hold values from -0.09375 to 0.09375
- proj_out: bfloat16 [1, 14336, 64], P(None, ('tensor', 'group')), may hold values from -0.046875 to 0.046875
- queries: bfloat16 [4096, 4096], P(('parts', 'tensor', 'group'), 'dp'), parts along dimension 0, may hold values from -0.005859375 to 0.005859375
Outputs:
- scores: float32 [16, 4096], P('dp', ('parts', 'tensor', 'group')), parts along dimension 1
There are 2 independent parts, one for each index of `parts`. A program takes and returns all parts, laid end to end along the dimension named above; an argument that names none is the same for every part. Nothing has to cross between parts.
All inputs are finite; a program needn't handle non-finite values.
Results may differ from a plain program's by a relative error of at most 0.005.
Values may be sent and summed in bfloat16 or wider, within the bound.
A program may use at most 64 MiB of HBM per device.

v0:
```python
import jax
import jax.numpy as jnp
from jax import lax
from jax.sharding import PartitionSpec as P


def shards(activations, out_grads, proj_in, proj_out, queries):
    proj_acts = jnp.einsum(
        "lsth,lhr->lstr", activations, proj_in, preferred_element_type=jnp.float32
    )
    proj_grads = jnp.einsum(
        "lsth,lhr->lstr", out_grads, proj_out, preferred_element_type=jnp.float32
    )
    summed_acts, summed_grads = lax.psum((proj_acts, proj_grads), ("tensor", "group"))
    outer = jnp.einsum(
        "lsta,lstb->slab",
        summed_grads.astype(jnp.bfloat16),
        summed_acts.astype(jnp.bfloat16),
        preferred_element_type=jnp.float32,
    )
    seq_count = outer.shape[0]
    example_grads = outer.reshape(seq_count, -1).astype(jnp.bfloat16)
    traded = lax.all_to_all(example_grads, "dp", split_axis=1, concat_axis=0, tiled=True)
    return lax.psum_scatter(
        lax.dot_general(
            traded, queries, (((1,), (1,)), ((), ())), preferred_element_type=jnp.float32
        ),
        "dp",
        scatter_dimension=0,
        tiled=True,
    )


def solution(mesh):
    placed = (
        P(None, ("parts", "dp"), None, ("tensor", "group")),
        P(None, ("parts", "dp"), None, ("tensor", "group")),
        P(None, ("tensor", "group"), None),
        P(None, ("tensor", "group"), None),
        P(("parts", "tensor", "group"), "dp"),
    )
    return jax.shard_map(
        shards,
        mesh=mesh,
        in_specs=placed,
        out_specs=P("dp", ("parts", "tensor", "group")),
        check_vma=False,
    )
```

profile of v0, /device:TPU:0, one launch (start us, length us, event | category | flops | bytes accessed | tf_op | source)
XLA Modules:
  0.0 57.4 jit_solution(16096773874334835234)
XLA Ops:
  0.0 0.0 copy-start
  0.0 0.0 copy-start.1
  0.0 1.6 %copy-done = bf16[1,4,256,1024]{3,2,1,0:T(8,128)(2,1)S(1)} copy-done((bf16[1,4,256,1024]{3,2,1,0:T(8,128)(2,1)S(1)}, bf16[1,4,256,1024]{3,2,1,0:T(8,128)(2,1)}, u32[]{:S(2)}) %copy-start) | copy-done | bytes 2097176
  1.6 1.7 %fusion.4 = f32[1,4,256,64]{2,3,1,0:T(8,128)S(1)} fusion(bf16[1,4,256,1024]{3,2,1,0:T(8,128)(2,1)S(1)} %copy-done, bf16[1,1024,64]{1,2,0:T(8,128)(2,1)} %param.7), kind=kOutput, calls=%fused_computation.4 | convolution fusion | flops 134217728 | bytes 2490368 | tf_op jit(solution)/shard_map/lsth,lhr->lstr/dot_general | solution.py:8
  3.3 5.5 %fusion.7 = f32[1,4,256,64]{2,3,1,0:T(8,128)S(1)} fusion(bf16[1,4,256,3584]{3,2,1,0:T(8,128)(2,1)} %param.6, bf16[1,3584,64]{1,2,0:T(8,128)(2,1)} %param.8), kind=kOutput, calls=%fused_computation.5 | convolution fusion | flops 469762048 | bytes 8060928 | tf_op jit(solution)/shard_map/lsth,lhr->lstr/dot_general | solution.py:11
  8.7 18.7 %all-reduce.3 = (bf16[1,4,256,64]{2,3,1,0:T(8,128)(2,1)S(1)}, bf16[1,4,256,64]{2,3,1,0:T(8,128)(2,1)S(1)}) all-reduce(f32[1,4,256,64]{2,3,1,0:T(8,128)S(1)} %fusion.4, f32[1,4,256,64]{2,3,1,0:T(8,128)S(1)} %fusion.7), channel_id=1, replica_groups=mesh['parts'=2,'dp'=4,'tensor'=2,'group'=2] {'tensor','group'}, use_global_device_ids=true, to_apply=%region_1.0 | all-reduce | flops 131072 | bytes 786432 | tf_op jit(solution)/shard_map/psum | solution.py:14
  27.4 0.2 convolution_convert_fusion
  27.6 0.1 convert_element_type.16
  27.7 0.6 %copy.7 = bf16[4,4,1024]{2,0,1:T(4,128)(2,1)} copy(bf16[4,4,1024]{2,1,0:T(4,128)(2,1)S(1)} %convert_element_type.16) | data formatting | bytes 65536 | tf_op jit(solution)/shard_map/convert_element_type | solution.py:22
  28.3 4.9 %all-to-all-start = ((bf16[4,4,1024]{2,0,1:T(4,128)(2,1)}), bf16[4,4,1024]{2,0,1:T(4,128)(2,1)S(1)}, u32[]{:S(2)}, u32[]{:S(2)}) async-start(bf16[4,4,1024]{2,0,1:T(4,128)(2,1)} %copy.7), calls=%async_computation | async-start | bytes 65536 | tf_op jit(solution)/shard_map/all_to_all | solution.py:23
  33.1 0.0 copy-done.1
  33.1 0.6 %dynamic-slice = u32[1]{0:T(128)} dynamic-slice(u32[32]{0:T(128)S(1)} %copy-done.1, u32[]{:T(128)S(6)} %add.7), dynamic_slice_sizes={1} | dynamic-slice | bytes 12
  34.4 4.4 %all-to-all-done = bf16[4,4,1024]{2,0,1:T(4,128)(2,1)S(1)} async-done(((bf16[4,4,1024]{2,0,1:T(4,128)(2,1)}), bf16[4,4,1024]{2,0,1:T(4,128)(2,1)S(1)}, u32[]{:S(2)}, u32[]{:S(2)}) %all-to-all-start) | async-done | bytes 32800 | tf_op jit(solution)/shard_map/all_to_all | solution.py:23
  38.8 1.6 %fusion.16 = f32[16,512]{1,0:T(8,128)S(1)} fusion(bf16[16,1024]{1,0:T(8,128)(2,1)S(1)} %all_to_all.14, bf16[512,1024]{1,0:T(8,128)(2,1)} %param.9), kind=kOutput, calls=%fused_computation.14 | convolution fusion | flops 16777216 | bytes 1114112 | tf_op jit(solution)/shard_map/dot_general | solution.py:25
  40.4 16.4 %all-reduce = f32[16,512]{1,0:T(8,128)S(1)} all-reduce(f32[16,512]{1,0:T(8,128)S(1)} %fusion.16), channel_id=2, replica_groups=mesh['parts'=2,'dp'=4,'tensor'=2,'group'=2] {'dp'}, use_global_device_ids=true, to_apply=%region_2.0.clone | all-reduce | flops 8192 | bytes 65536
  56.8 0.6 %constant_dynamic-slice_fusion = f32[4,512]{1,0:T(4,128)} fusion(f32[16,512]{1,0:T(8,128)S(1)} %all-reduce, u32[]{:T(128)S(6)} %multiply.1), kind=kLoop, calls=%fused_computation.13 | loop fusion | bytes 16388
  (1 shorter events, 0.0 us)
Async XLA Ops:
  0.0 1.6 %copy-start = (bf16[1,4,256,1024]{3,2,1,0:T(8,128)(2,1)S(1)}, bf16[1,4,256,1024]{3,2,1,0:T(8,128)(2,1)}, u32[]{:S(2)}) copy-start(bf16[1,4,256,1024]{3,2,1,0:T(8,128)(2,1)} %param.5) | copy-start | bytes 6291460
  0.0 33.1 %copy-start.1 = (u32[32]{0:T(128)S(1)}, u32[32]{0:T(128)}, u32[]{:S(2)}) copy-start(u32[32]{0:T(128)} %constant.4) | copy-start | bytes 388
  28.3 10.5 %all-to-all-start = ((bf16[4,4,1024]{2,0,1:T(4,128)(2,1)}), bf16[4,4,1024]{2,0,1:T(4,128)(2,1)S(1)}, u32[]{:S(2)}, u32[]{:S(2)}) async-start(bf16[4,4,1024]{2,0,1:T(4,128)(2,1)} %copy.7), calls=%async_computation | async-start | bytes 65536 | tf_op jit(solution)/shard_map/all_to_all | solution.py:23
where the time goes:
time: 57.8 us; the launch traced here: 57.4 us
  blocking collectives  35.1 us (61%)
  matrix products  8.89 us (15%)
  starting transfers between devices  4.86 us (8%)
  waiting for transfers between devices  4.42 us (8%)
  local copies, waits for them, and re-layouts  3.53 us (6%)
  between operations  0.69 us (1%)
    psum x1, blocking collectives, shards(): lax.psum((proj_acts, proj_grads), ('tensor', 'group'))  18.7 us
    unnamed x1, blocking collectives  16.4 us
    dot_general x1, matrix products, shards(): jnp.einsum('lsth,lhr->lstr', out_grads, proj_out, preferred_element_type=...  5.46 us
    all_to_all x1, starting transfers between devices, shards(): lax.all_to_all(example_grads, 'dp', split_axis=1, concat_axis=0, tiled=True)  4.86 us
    all_to_all x1, waiting for transfers between devices, shards(): lax.all_to_all(example_grads, 'dp', split_axis=1, concat_axis=0, tiled=True)  4.42 us
    unnamed x6, local copies, waits for them, and re-layouts  2.78 us
    dot_general x1, matrix products, shards(): jnp.einsum('lsth,lhr->lstr', activations, proj_in, preferred_element_type...  1.66 us
    dot_general x1, matrix products, shards(): lax.dot_general(traded, queries, (((1,), (1,)), ((), ())), preferred_elem...  1.6 us
  transfers between devices with their start and end apart: 1, of which 1 were waited for; matrix products, arithmetic and copies ran while one was open for 1% of the time, Pallas kernels for 0%

commit v1 on v0

--- a/solution.py
+++ b/solution.py
@@ -1,7 +1,17 @@
+import functools
+import itertools
+
 import jax
 import jax.numpy as jnp
 from jax import lax
+from jax.experimental import pallas as pl
+from jax.experimental.pallas import tpu as pltpu
 from jax.sharding import PartitionSpec as P
+
+MESH = pl.DeviceIdType.MESH
+WIRE = jnp.bfloat16
+NT = (((1,), (1,)), ((), ()))
+LANES = 128
 
 
 def shards(activations, out_grads, proj_in, proj_out, queries):
@@ -31,6 +41,196 @@
     )
 
 
+def dot(left, right):
+    return lax.dot_general(left, right, NT, preferred_element_type=jnp.float32)
+
+
+def kernel(
+    sizes,
+    acts_hbm, grads_hbm, in_hbm, out_hbm, queries_hbm, scores_ref,
+    acts, grads, w_in, w_out, queries, paired, own, sent, got, mine, feats, part, back,
+    load_sem, send1, recv1, send2, recv2, send3, recv3,
+):
+    nd, nt, ng = sizes
+    seqs, rank = nt * ng, w_in.shape[0]
+    half = rank // 2
+    d, t, g = lax.axis_index("dp"), lax.axis_index("tensor"), lax.axis_index("group")
+
+    def peer(rd, rt, rg):
+        return lax.rem(d + rd, nd), lax.rem(t + rt, nt), lax.rem(g + rg, ng)
+
+    def device(where):
+        return {"dp": where[0], "tensor": where[1], "group": where[2]}
+
+    turns = sorted(itertools.product(range(nt), range(ng)), reverse=True)
+    others = [r for r in itertools.product(range(nd), range(nt), range(ng)) if any(r)]
+    others.sort(key=lambda r: (-min(r[0], nd - r[0]), -r[1], -r[2]))
+
+    loads = [
+        pltpu.make_async_copy(in_hbm, w_in, load_sem.at[0]),
+        pltpu.make_async_copy(out_hbm, w_out, load_sem.at[1]),
+    ]
+    seq_loads = []
+    for slot, (rt, rg) in enumerate(turns):
+        _, pt, pg = peer(0, rt, rg)
+        seq = pt * ng + pg
+        seq_loads.append((
+            pltpu.make_async_copy(acts_hbm.at[0, seq], acts.at[slot], load_sem.at[3 + 2 * slot]),
+            pltpu.make_async_copy(grads_hbm.at[0, seq], grads.at[slot], load_sem.at[4 + 2 * slot]),
+        ))
+    query_load = pltpu.make_async_copy(queries_hbm, queries, load_sem.at[2])
+    for copy in loads:
+        copy.start()
+    for pair in seq_loads:
+        for copy in pair:
+            copy.start()
+    query_load.start()
+
+    barrier = pltpu.get_barrier_semaphore()
+    for r in others:
+        pl.semaphore_signal(barrier, inc=1, device_id=device(peer(*r)), device_id_type=MESH)
+
+    row = lax.broadcasted_iota(jnp.int32, (rank, rank), 0)
+    column = lax.broadcasted_iota(jnp.int32, (rank, rank), 1)
+    source = jnp.where(row < half, 2 * row, 2 * (row - half) + 1)
+    pick = (column == source).astype(jnp.bfloat16)
+    loads[1].wait()
+    paired[...] = jnp.dot(
+        pick, w_out[...], preferred_element_type=jnp.float32
+    ).astype(jnp.bfloat16)
+    loads[0].wait()
+
+    first = []
+    for slot, (rt, rg) in enumerate(turns):
+        seq_loads[slot][0].wait()
+        part_acts = dot(w_in[...], acts[slot])
+        seq_loads[slot][1].wait()
+        part_grads = dot(paired[...], grads[slot])
+        if (rt, rg) == (0, 0):
+            own[:rank] = part_acts
+            own[rank:] = part_grads
+            continue
+        sent[slot, :rank] = part_acts.astype(sent.dtype)
+        sent[slot, rank:] = part_grads.astype(sent.dtype)
+        if not first:
+            pl.semaphore_wait(barrier, len(others))
+        copy = pltpu.make_async_remote_copy(
+            src_ref=sent.at[slot],
+            dst_ref=got.at[slot],
+            send_sem=send1.at[slot],
+            recv_sem=recv1.at[slot],
+            device_id=device(peer(0, rt, rg)),
+            device_id_type=MESH,
+        )
+        copy.start()
+        first.append(copy)
+
+    total = own[...]
+    for slot, copy in enumerate(first):
+        copy.wait_recv()
+        total = total + got[slot].astype(jnp.float32)
+    summed = total.astype(jnp.bfloat16)
+    twice = jnp.concatenate([summed[:rank], summed[:rank]], axis=0)
+    outer = dot(summed[rank:], twice)
+    lane = lax.broadcasted_iota(jnp.int32, (half, 2 * rank), 1)
+    eg = jnp.where(lane < rank, outer[:half], outer[half:])
+    eg = eg.astype(jnp.bfloat16).astype(jnp.float32)
+    deep = half // nd
+    for other in range(nd):
+        mine[other] = eg[other * deep:(other + 1) * deep]
+
+    me = (d * nt + t) * ng + g
+    second = []
+    for at, r in enumerate(others):
+        where = peer(*r)
+        copy = pltpu.make_async_remote_copy(
+            src_ref=mine.at[where[0]],
+            dst_ref=feats.at[me],
+            send_sem=send2.at[at],
+            recv_sem=recv2.at[at],
+            device_id=device(where),
+            device_id_type=MESH,
+        )
+        copy.start()
+        second.append(copy)
+    feats[me] = mine[d]
+    query_load.wait()
+    for copy in second:
+        copy.wait_recv()
+    flat = jnp.concatenate([feats[:, k, :] for k in range(deep)], axis=1).astype(jnp.bfloat16)
+    scores = dot(flat, queries[...])
+    for other in range(nd):
+        part[other] = scores[other * seqs:(other + 1) * seqs]
+
+    third = []
+    for rd in sorted(range(1, nd), key=lambda r: -min(r, nd - r)):
+        where = peer(rd, 0, 0)
+        copy = pltpu.make_async_remote_copy(
+            src_ref=part.at[where[0]],
+            dst_ref=back.at[rd - 1],
+            send_sem=send3.at[rd - 1],
+            recv_sem=recv3.at[rd - 1],
+            device_id=device(where),
+            device_id_type=MESH,
+        )
+        copy.start()
+        third.append((rd, copy))
+    result = part[d]
+    for rd, copy in reversed(third):
+        copy.wait_recv()
+        result = result + back[rd - 1]
+    scores_ref[...] = result
+    for copy in first + second + [copy for _, copy in third]:
+        copy.wait_send()
+
+
+def fused(sizes, activations, out_grads, proj_in, proj_out, queries):
+    nd, nt, ng = sizes
+    seqs, tokens, width = activations.shape[1:]
+    hidden, rank = out_grads.shape[3], proj_in.shape[2]
+    asked, local = queries.shape
+    everyone = nd * seqs
+    deep = rank // 2 // nd
+    bf16, f32 = jnp.bfloat16, jnp.float32
+    dma = pltpu.SemaphoreType.DMA
+    hbm = pl.BlockSpec(memory_space=pl.ANY)
+    return pl.pallas_call(
+        functools.partial(kernel, sizes),
+        out_shape=jax.ShapeDtypeStruct((seqs, asked), f32),
+        in_specs=[hbm] * 5,
+        out_specs=pl.BlockSpec(memory_space=pltpu.VMEM),
+        scratch_shapes=[
+            pltpu.VMEM((seqs, tokens, width), bf16),
+            pltpu.VMEM((seqs, tokens, hidden), bf16),
+            pltpu.VMEM((rank, width), bf16),
+            pltpu.VMEM((rank, hidden), bf16),
+            pltpu.VMEM((asked, local), bf16),
+            pltpu.VMEM((rank, hidden), bf16),
+            pltpu.VMEM((2 * rank, tokens), f32),
+            pltpu.VMEM((seqs, 2 * rank, tokens), WIRE),
+            pltpu.VMEM((seqs, 2 * rank, tokens), WIRE),
+            pltpu.VMEM((nd, deep, LANES), f32),
+            pltpu.VMEM((everyone, deep, LANES), f32),
+            pltpu.VMEM((nd, seqs, asked), f32),
+            pltpu.VMEM((nd, seqs, asked), f32),
+            dma((3 + 2 * seqs,)),
+            dma((seqs,)), dma((seqs,)),
+            dma((everyone,)), dma((everyone,)),
+            dma((nd,)), dma((nd,)),
+        ],
+        compiler_params=pltpu.CompilerParams(
+            collective_id=0, has_side_effects=True, vmem_limit_bytes=60 * 2**20
+        ),
+        name="scores",
+    )(
+        activations,
+        out_grads,
+        jnp.swapaxes(proj_in[0], 0, 1),
+        jnp.swapaxes(proj_out[0], 0, 1),
+        queries,
+    )
+
+
 def solution(mesh):
     placed = (
         P(None, ("parts", "dp"), None, ("tensor", "group")),
@@ -39,8 +239,22 @@
         P(None, ("tensor", "group"), None),
         P(("parts", "tensor", "group"), "dp"),
     )
+    sizes = mesh.shape["dp"], mesh.shape["tensor"], mesh.shape["group"]
+
+    def body(activations, out_grads, proj_in, proj_out, queries):
+        layers, seqs = activations.shape[:2]
+        rank = proj_in.shape[2]
+        fits = (
+            layers == 1
+            and seqs == sizes[1] * sizes[2]
+            and 2 * rank == LANES
+            and rank % (2 * sizes[0]) == 0
+        )
+        run = functools.partial(fused, sizes) if fits else shards
+        return run(activations, out_grads, proj_in, proj_out, queries)
+
     return jax.shard_map(
-        shards,
+        body,
         mesh=mesh,
         in_specs=placed,
         out_specs=P("dp", ("parts", "tensor", "group")),

time: 57.8 us -> 22.3 us (0.39)
  blocking collectives: 35.1 us -> 0 us
  Pallas kernels: 0 us -> 20.8 us
  matrix products: 8.89 us -> 0 us
  starting transfers between devices: 4.86 us -> 0 us
  waiting for transfers between devices: 4.42 us -> 0 us
  local copies, waits for them, and re-layouts: 3.53 us -> 1.3 us
  between operations: 0.69 us -> 0.01 us
    pallas_call x0 -> x1, Pallas kernels: none -> 20.8 us  [fused(): pl.pallas_call(functools.partial(kernel, sizes), out_shape=jax.ShapeDtype...]
    psum x1 -> x0, blocking collectives: 18.7 us -> none  [shards(): lax.psum((proj_acts, proj_grads), ('tensor', 'group'))]
    unnamed x1 -> x0, blocking collectives: 16.4 us -> none
    dot_general x4 -> x0, matrix products: 8.89 us -> none  [the longest x1 5.46 us: shards(): jnp.einsum('lsth,lhr->lstr', out_grads, proj_out, preferred_element_type=...]
    all_to_all x1 -> x0, starting transfers between devices: 4.86 us -> none  [shards(): lax.all_to_all(example_grads, 'dp', split_axis=1, concat_axis=0, tiled=True)]
    all_to_all x1 -> x0, waiting for transfers between devices: 4.42 us -> none  [shards(): lax.all_to_all(example_grads, 'dp', split_axis=1, concat_axis=0, tiled=True)]
    unnamed x6 -> x1, local copies, waits for them, and re-layouts: 2.78 us -> 1.3 us
    convert_element_type x2 -> x0, local copies, waits for them, and re-layouts: 0.73 us -> none  [shards(): example_grads = outer.reshape(seq_count, -1).astype(jnp.bfloat16)]
  transfers between devices with their start and end apart: 1 -> 0, of which waited for: 1 -> 0; matrix products, arithmetic and copies ran while one was open for 1% -> 0% of each run, Pallas kernels for 0% -> 0%
where the time goes in v1:
time: 22.3 us; the launch traced here: 22.1 us
  Pallas kernels  20.8 us (93%)
  local copies, waits for them, and re-layouts  1.3 us (6%)
    pallas_call x1, Pallas kernels, fused(): pl.pallas_call(functools.partial(kernel, sizes), out_shape=jax.ShapeDtype...  20.8 us
    unnamed x1, local copies, waits for them, and re-layouts  1.3 us

profile of v1, /device:TPU:0, one launch (start us, length us, event | category | flops | bytes accessed | tf_op | source)
XLA Modules:
  0.0 22.1 jit_solution(2157160187716335430)
XLA Ops:
  0.0 20.8 %scores.1 = f32[4,512]{1,0:T(4,128)} custom-call(bf16[1,4,256,1024]{3,2,1,0:T(8,128)(2,1)} %acts_hbm.1, bf16[1,4,256,3584]{3,2,1,0:T(8,128)(2,1)} %grads_hbm.1, bf16[64,1024]{1,0:T(8,128)(2,1)} %bitcast.7, bf16[64,3584]{1,0:T(8,128)(2,1)} %bitcast.6, bf16[512,1024]{1,0:T(8,128)(2,1)} %queries_hbm.1), custom_call_target="tpu_custom_call" | custom-call | tf_op jit(solution)/shard_map/scores/pallas_call | solution.py:197
  20.8 1.3 %copy.7 = f32[4,512]{1,0:T(4,128)} copy(f32[4,512]{1,0:T(4,128)} %scores.1) | data formatting | bytes 16384

commit v2 on v1

--- a/solution.py
+++ b/solution.py
@@ -79,16 +79,16 @@
             pltpu.make_async_copy(grads_hbm.at[0, seq], grads.at[slot], load_sem.at[4 + 2 * slot]),
         ))
     query_load = pltpu.make_async_copy(queries_hbm, queries, load_sem.at[2])
+    barrier = pltpu.get_barrier_semaphore()
+    for r in others:
+        pl.semaphore_signal(barrier, inc=1, device_id=device(peer(*r)), device_id_type=MESH)
+
     for copy in loads:
         copy.start()
     for pair in seq_loads:
         for copy in pair:
             copy.start()
     query_load.start()
-
-    barrier = pltpu.get_barrier_semaphore()
-    for r in others:
-        pl.semaphore_signal(barrier, inc=1, device_id=device(peer(*r)), device_id_type=MESH)
 
     row = lax.broadcasted_iota(jnp.int32, (rank, rank), 0)
     column = lax.broadcasted_iota(jnp.int32, (rank, rank), 1)
@@ -103,8 +103,8 @@
     first = []
     for slot, (rt, rg) in enumerate(turns):
         seq_loads[slot][0].wait()
+        seq_loads[slot][1].wait()
         part_acts = dot(w_in[...], acts[slot])
-        seq_loads[slot][1].wait()
         part_grads = dot(paired[...], grads[slot])
         if (rt, rg) == (0, 0):
             own[:rank] = part_acts
@@ -219,7 +219,7 @@
             dma((nd,)), dma((nd,)),
         ],
         compiler_params=pltpu.CompilerParams(
-            collective_id=0, has_side_effects=True, vmem_limit_bytes=60 * 2**20
+            collective_id=0, has_side_effects=True, vmem_limit_bytes=56_500_000
         ),
         name="scores",
     )(

time: 22.3 us -> 20.8 us (0.933)
  local copies, waits for them, and re-layouts: 1.3 us -> 0.6 us
  Pallas kernels: 20.8 us -> 20.1 us
    pallas_call x1, Pallas kernels: 20.8 us -> 20.1 us  [fused(): pl.pallas_call(functools.partial(kernel, sizes), out_shape=jax.ShapeDtype...]
    unnamed x1, local copies, waits for them, and re-layouts: 1.3 us -> 0.6 us
where the time goes in v2:
time: 20.8 us; the launch traced here: 20.7 us
  Pallas kernels  20.1 us (97%)
  local copies, waits for them, and re-layouts  0.6 us (3%)
    pallas_call x1, Pallas kernels, fused(): pl.pallas_call(functools.partial(kernel, sizes), out_shape=jax.ShapeDtype...  20.1 us
    unnamed x1, local copies, waits for them, and re-layouts  0.6 us

profile of v2, /device:TPU:0, one launch (start us, length us, event | category | flops | bytes accessed | tf_op | source)
XLA Modules:
  0.0 20.7 jit_solution(2808556710484395280)
XLA Ops:
  0.0 20.1 %scores.1 = f32[4,512]{1,0:T(4,128)S(1)} custom-call(bf16[1,4,256,1024]{3,2,1,0:T(8,128)(2,1)} %acts_hbm.1, bf16[1,4,256,3584]{3,2,1,0:T(8,128)(2,1)} %grads_hbm.1, bf16[64,1024]{1,0:T(8,128)(2,1)} %bitcast.7, bf16[64,3584]{1,0:T(8,128)(2,1)} %bitcast.6, bf16[512,1024]{1,0:T(8,128)(2,1)} %queries_hbm.1), custom_call_target="tpu_custom_call" | custom-call | tf_op jit(solution)/shard_map/scores/pallas_call | solution.py:197
  20.1 0.6 %copy.7 = f32[4,512]{1,0:T(4,128)} copy(f32[4,512]{1,0:T(4,128)S(1)} %scores.1) | data formatting | bytes 16384

commit v3 on v2

--- a/solution.py
+++ b/solution.py
@@ -64,7 +64,7 @@
 
     turns = sorted(itertools.product(range(nt), range(ng)), reverse=True)
     others = [r for r in itertools.product(range(nd), range(nt), range(ng)) if any(r)]
-    others.sort(key=lambda r: (-min(r[0], nd - r[0]), -r[1], -r[2]))
+    others.sort(key=lambda r: (-r[0], -r[1], -r[2]))
 
     loads = [
         pltpu.make_async_copy(in_hbm, w_in, load_sem.at[0]),

time: 20.8 us -> 20.6 us (level)
  Pallas kernels: 20.1 us -> 19.8 us
    pallas_call x1, Pallas kernels: 20.1 us -> 19.8 us  [fused(): pl.pallas_call(functools.partial(kernel, sizes), out_shape=jax.ShapeDtype...]
where the time goes in v3:
time: 20.6 us; the launch traced here: 20.4 us
  Pallas kernels  19.8 us (96%)
  local copies, waits for them, and re-layouts  0.6 us (3%)
    pallas_call x1, Pallas kernels, fused(): pl.pallas_call(functools.partial(kernel, sizes), out_shape=jax.ShapeDtype...  19.8 us
    unnamed x1, local copies, waits for them, and re-layouts  0.6 us

profile of v3, /device:TPU:0, one launch (start us, length us, event | category | flops | bytes accessed | tf_op | source)
XLA Modules:
  0.0 20.4 jit_solution(17541871170989711474)
XLA Ops:
  0.0 19.8 %scores.1 = f32[4,512]{1,0:T(4,128)S(1)} custom-call(bf16[1,4,256,1024]{3,2,1,0:T(8,128)(2,1)} %acts_hbm.1, bf16[1,4,256,3584]{3,2,1,0:T(8,128)(2,1)} %grads_hbm.1, bf16[64,1024]{1,0:T(8,128)(2,1)} %bitcast.7, bf16[64,3584]{1,0:T(8,128)(2,1)} %bitcast.6, bf16[512,1024]{1,0:T(8,128)(2,1)} %queries_hbm.1), custom_call_target="tpu_custom_call" | custom-call | tf_op jit(solution)/shard_map/scores/pallas_call | solution.py:197
  19.8 0.6 %copy.7 = f32[4,512]{1,0:T(4,128)} copy(f32[4,512]{1,0:T(4,128)S(1)} %scores.1) | data formatting | bytes 16384
